TPU v7x, 32 devices: a whole 2x2x4 slice. The times are simulated.
32 devices in a mesh: dp: 8 (over z, core), tensor: 4 (over y, x).
Axes of the slice: x: 2, y: 2, z: 4, core: 2. Of those that a mesh axis runs over, the one named last changes fastest.
Arguments:
- tokens: bfloat16 [4096, 4096], P('dp', 'tensor'), may hold values from -6 to 6
- butterfly: bfloat16 [64, 5, 256, 256], P('tensor', None, 'dp'), may hold values from -0.15625 to 0.15625
- left_factor: bfloat16 [4096, 256], P(('tensor', 'dp')), may hold values from -0.09375 to 0.09375
- right_factor: bfloat16 [256, 16384], P('dp', 'tensor'), may hold values from -0.375 to 0.375
- cotangent: bfloat16 [4096, 16384], P('dp', 'tensor'), may hold values from -6 to 6
Outputs:
- hidden: bfloat16 [4096, 16384], P('dp', 'tensor')
- grad_tokens: bfloat16 [4096, 4096], P('dp', 'tensor')
- grad_butterfly: bfloat16 [64, 5, 256, 256], P('tensor', None, 'dp')
- grad_left: bfloat16 [4096, 256], P(('tensor', 'dp'))
- grad_right: bfloat16 [256, 16384], P('dp', 'tensor')
All inputs are finite; a program needn't handle non-finite values.
Results may differ from a plain program's by a relative error of at most 0.02.
Values may be sent and summed in bfloat16 or wider, within the bound.
A program may use at most 128 MiB of HBM per device.

v0:
```python
import jax
import jax.numpy as jnp
from jax import lax
from jax.sharding import PartitionSpec as P

BLK = 256
LOG = 4
ROOT_HALF = 0.7071067811865476
INV_ROOT_TWO_PI = 0.3989422804014327


def swapped(block, axis, stride):
    count = lax.axis_size(axis)
    route = []
    for low in range(count):
        high = low | 1 << stride
        if high != low and high < count:
            route += [(low, high), (high, low)]
    return lax.ppermute(block, axis, route)


def gelu_pair(preact):
    cdf = 0.5 * (1.0 + jax.scipy.special.erf(preact * ROOT_HALF))
    return (preact * cdf, cdf + preact * INV_ROOT_TWO_PI * jnp.exp(-0.5 * preact * preact))


def flip_blocks(blocks, stride):
    full_shape = blocks.shape
    leading = full_shape[:-2]
    block_count = full_shape[-2]
    halves = blocks.reshape(leading + (block_count // (2 * stride), 2, stride, full_shape[-1]))
    return jnp.flip(halves, axis=-3).reshape(full_shape)


def per_device(tokens, butterfly, left_factor, right_factor, cotangent):
    rows_here = tokens.shape[0]
    blocks_here = tokens.shape[1] // BLK
    shift_bits = blocks_here.bit_length() - 1
    hidden_blocks = right_factor.shape[1] // BLK
    group_ratio = hidden_blocks // blocks_here
    weights, left_full, right_full = (
        lax.all_gather(butterfly, "dp", axis=2, tiled=True),
        lax.all_gather(left_factor, "dp", axis=0, tiled=True),
        lax.all_gather(right_factor, "dp", axis=0, tiled=True),
    )
    blocks = tokens.reshape(rows_here, blocks_here, BLK)
    partners = [blocks]
    for level in range(LOG):
        if 1 << level < blocks_here:
            partners.append(flip_blocks(blocks, 1 << level))
        else:
            partners.append(swapped(blocks, "tensor", level - shift_bits))
    stacked = jnp.stack(partners)
    weight_blocks = weights.reshape(blocks_here, group_ratio, LOG + 1, BLK, BLK)
    preact = jnp.einsum(
        "ktqi,qrkio->tqro", stacked, weight_blocks, preferred_element_type=jnp.float32
    )
    preact = preact.reshape(rows_here, hidden_blocks * BLK)
    low_part = jnp.dot(tokens, left_full, preferred_element_type=jnp.float32)
    low_rank = lax.psum(low_part.astype(jnp.bfloat16), "tensor")
    preact = preact + jnp.dot(low_rank, right_full, preferred_element_type=jnp.float32)
    activation, slopes = gelu_pair(preact)
    hidden = activation.astype(jnp.bfloat16)
    grad_pre = (cotangent.astype(jnp.float32) * slopes).astype(jnp.bfloat16)
    grad_wide = grad_pre.reshape(rows_here, blocks_here, group_ratio, BLK)
    grad_weight = jnp.einsum(
        "ktqi,tqro->qrkio", stacked, grad_wide, preferred_element_type=jnp.float32
    )
    grad_weight = grad_weight.reshape(hidden_blocks, LOG + 1, BLK, BLK)
    low_back = jnp.einsum("th,rh->tr", grad_pre, right_full, preferred_element_type=jnp.float32)
    grad_low = lax.psum(low_back.astype(jnp.bfloat16), "tensor")
    grad_first = jnp.einsum("td,tr->dr", tokens, grad_low, preferred_element_type=jnp.float32)
    grad_second = jnp.einsum("tr,th->rh", low_rank, grad_pre, preferred_element_type=jnp.float32)
    returned = jnp.einsum(
        "tqro,qrkio->ktqi", grad_wide, weight_blocks, preferred_element_type=jnp.float32
    )
    summed = returned[0]
    for level in range(LOG):
        contrib = returned[level + 1]
        if 1 << level < blocks_here:
            summed = summed + flip_blocks(contrib, 1 << level)
        else:
            summed = summed + swapped(
                contrib.astype(jnp.bfloat16), "tensor", level - shift_bits
            ).astype(contrib.dtype)
    grad_input = summed.reshape(rows_here, blocks_here * BLK)
    grad_input = grad_input + jnp.einsum(
        "tr,dr->td", grad_low, left_full, preferred_element_type=jnp.float32
    )
    sum_weight, sum_first, sum_second = (
        lax.psum_scatter(
            grad_weight.astype(jnp.bfloat16), "dp", scatter_dimension=2, tiled=True
        ).astype(jnp.float32),
        lax.psum_scatter(
            grad_first.astype(jnp.bfloat16), "dp", scatter_dimension=0, tiled=True
        ).astype(jnp.float32),
        lax.psum_scatter(
            grad_second.astype(jnp.bfloat16), "dp", scatter_dimension=0, tiled=True
        ).astype(jnp.float32),
    )
    return (
        hidden,
        grad_input.astype(jnp.bfloat16),
        sum_weight.astype(jnp.bfloat16),
        sum_first.astype(jnp.bfloat16),
        sum_second.astype(jnp.bfloat16),
    )


def solution(mesh):
    placed = (
        P("dp", "tensor"),
        P("tensor", None, "dp", None),
        P(("tensor", "dp"), None),
        P("dp", "tensor"),
        P("dp", "tensor"),
    )
    return jax.shard_map(
        per_device,
        mesh=mesh,
        in_specs=placed,
        out_specs=(
            P("dp", "tensor"),
            P("dp", "tensor"),
            P("tensor", None, "dp", None),
            P(("tensor", "dp"), None),
            P("dp", "tensor"),
        ),
        check_vma=False,
    )
```

profile of v0, /device:TPU:0, one launch (start us, length us, event | category | flops | bytes accessed | tf_op | source)
XLA Modules:
  0.0 386.7 jit_solution(5141714083734337590)
XLA Ops:
  8.8 16.8 %all_gather.10 = bf16[1024,256]{1,0:T(8,128)(2,1)S(1)} all-gather(bf16[128,256]{1,0:T(8,128)(2,1)} %param.7), channel_id=1, replica_groups=mesh['dp'=8,'tensor'=4] {'dp'}, dimensions={0}, use_global_device_ids=true | all-gather | bytes 589824 | tf_op jit(solution)/shard_map/all_gather | solution.py:43
  26.4 2.4 convolution_convert_fusion.4
  39.1 2.3 copy.42
  42.8 2.4 copy.41
  45.2 2.3 rev.16
  48.5 2.3 constant_dynamic-update-slice_fusion.1
  51.8 8.5 %collective-permute-done = bf16[512,4,256]{2,0,1:T(8,128)(2,1)} collective-permute-done((bf16[512,4,256]{2,0,1:T(8,128)(2,1)}, bf16[512,4,256]{2,0,1:T(8,128)(2,1)}, u32[]{:S(2)}, u32[]{:S(2)}) %collective-permute-start) | collective-permute-done | bytes 1048608 | tf_op jit(solution)/shard_map/ppermute | solution.py:19
  60.3 2.3 bitcast_dynamic-update-slice_fusion.1
  62.6 2.3 bitcast_dynamic-update-slice_fusion
  64.8 47.8 %all-gather.3.cloned.1.call-done = bf16[16,5,256,256]{3,2,1,0:T(8,128)(2,1)} async-done(((bf16[16,5,32,256]{3,2,1,0:T(8,128)(2,1)}), bf16[16,5,256,256]{3,2,1,0:T(8,128)(2,1)}) %all-gather.3.cloned.1.call-update) | async-done | bytes 10485776 | tf_op jit(solution)/shard_map/all_gather | solution.py:42
  112.6 11.9 %fusion.6 = f32[4,512,4,256,1]{1,3,4,2,0:T(8,128)} fusion(bf16[4,4,5,256,256]{4,3,2,1,0:T(8,128)(2,1)} %bitcast.93, bf16[5,512,4,256]{3,1,0,2:T(8,128)(2,1)} %bitcast_dynamic-update-slice_fusion), kind=kOutput, calls=%fused_computation.11 | convolution fusion | flops 5368709120 | bytes 24117248 | tf_op jit(solution)/shard_map/ktqi,qrkio->tqro/dot_general | solution.py:55
  124.5 9.0 %copy.48 = f32[512,4096]{1,0:T(8,128)} copy(f32[512,4096]{0,1:T(8,128)} %bitcast.88) | data formatting | bytes 16777216 | tf_op jit(solution)/shard_map/reshape | solution.py:58
  133.5 8.6 %all-gather.5.cloned.1.call-done = bf16[256,4096]{1,0:T(8,128)(2,1)} async-done(((bf16[32,4096]{1,0:T(8,128)(2,1)}), bf16[256,4096]{1,0:T(8,128)(2,1)}) %all-gather.5.cloned.1.call-update) | async-done | bytes 2097168 | tf_op jit(solution)/shard_map/all_gather | solution.py:44
  142.1 10.0 %fusion.4 = (bf16[512,4096]{1,0:T(8,128)(2,1)S(1)}, bf16[512,4096]{1,0:T(8,128)(2,1)}) fusion(bf16[512,4096]{1,0:T(8,128)(2,1)} %param.9, f32[512,4096]{1,0:T(8,128)} %copy.48, bf16[512,256]{1,0:T(8,128)(2,1)} %all-reduce.3.cloned.1.call-done, bf16[256,4096]{1,0:T(8,128)(2,1)} %all-gather.5.cloned.1.call-done), kind=kOutput, calls=%fused_computation.5 | convolution fusion | flops 1103101952 | bytes 23330816 | tf_op jit(solution)/shard_map/dot_general | solution.py:61
  152.1 2.1 copy-done.1
  154.2 2.0 convolution_convert_fusion.3
  156.3 42.0 %all-reduce.5.cloned.1.call-done = bf16[512,256]{1,0:T(8,128)(2,1)} async-done(((bf16[512,256]{1,0:T(8,128)(2,1)}), bf16[512,256]{1,0:T(8,128)(2,1)}) %all-reduce.5.cloned.1.call-update) | async-done | bytes 262160 | tf_op jit(solution)/shard_map/psum | solution.py:71
  200.9 4.8 %convolution_convert_fusion.1 = bf16[256,4096]{1,0:T(8,128)(2,1)} fusion(bf16[512,256]{1,0:T(8,128)(2,1)S(1)} %copy-done.6, bf16[512,4096]{1,0:T(8,128)(2,1)} %copy-done.1), kind=kOutput, calls=%fused_computation.13 | convolution fusion | flops 1074790400 | bytes 6553600 | tf_op jit(solution)/shard_map/tr,th->rh/dot_general | solution.py:73
  205.8 7.9 %reshape.38 = bf16[512,4,4,256]{3,2,1,0:T(4,128)(2,1)} reshape(bf16[512,4096]{1,0:T(8,128)(2,1)} %copy-done.1) | data formatting | bytes 8388608 | tf_op jit(solution)/shard_map/reshape | solution.py:65
  213.7 7.5 %copy.62 = bf16[512,4,4,256,1]{0,3,4,2,1:T(8,128)(2,1)} copy(bf16[512,4,4,256,1]{3,2,1,0,4:T(4,128)(2,1)} %bitcast.83) | data formatting | bytes 8388608 | tf_op jit(solution)/shard_map/reshape | solution.py:65
  221.2 11.3 %convolution_convert_fusion = bf16[4,4,256,5,256]{4,2,3,1,0:T(8,128)(2,1)} fusion(bf16[512,4,4,256,1]{0,3,4,2,1:T(8,128)(2,1)} %copy.62, bf16[5,512,4,256]{3,1,0,2:T(8,128)(2,1)} %bitcast_dynamic-update-slice_fusion), kind=kOutput, calls=%fused_computation.9 | convolution fusion | flops 5373952000 | bytes 19922944 | tf_op jit(solution)/shard_map/ktqi,tqro->qrkio/dot_general | solution.py:66
  232.4 15.2 %copy.55 = bf16[16,5,256,256]{3,2,1,0:T(8,128)(2,1)} copy(bf16[16,5,256,256]{2,3,1,0:T(8,128)(2,1)} %bitcast.84) | data formatting | bytes 20971520 | tf_op jit(solution)/shard_map/convert_element_type | solution.py:92
  247.6 12.8 %fusion.14 = (bf16[5,512,4,256]{1,3,0,2:T(8,128)(2,1)}, f32[5,512,4,256]{1,3,0,2:T(8,128)}) fusion(bf16[512,4,4,256,1]{0,3,4,2,1:T(8,128)(2,1)} %copy.62, bf16[4,4,5,256,256]{4,3,2,1,0:T(8,128)(2,1)} %bitcast.94), kind=kOutput, calls=%fused_computation.33 | convolution fusion | flops 5371330560 | bytes 30408704 | tf_op jit(solution)/shard_map/tqro,qrkio->ktqi/dot_general | solution.py:74
  260.4 3.1 slice_bitcast_fusion.2
  265.6 4.7 %fusion.13 = (f32[1,512,4,256]{1,3,0,2:T(8,128)}, f32[1,512,4,256]{1,3,0,2:T(8,128)}) fusion(f32[5,512,4,256]{1,3,0,2:T(8,128)} %get-tuple-element.27), kind=kLoop, calls=%fused_computation.32 | loop fusion | bytes 8388608 | tf_op jit(solution)/shard_map/slice | solution.py:79
  270.2 1.8 rev.18
  272.0 3.1 rev.19
  276.9 11.3 %collective-permute-done.2 = bf16[512,4,256]{0,2,1:T(8,128)(2,1)} collective-permute-done((bf16[512,4,256]{0,2,1:T(8,128)(2,1)}, bf16[512,4,256]{0,2,1:T(8,128)(2,1)}, u32[]{:S(2)}, u32[]{:S(2)}) %collective-permute-start.2) | collective-permute-done | bytes 1048608 | tf_op jit(solution)/shard_map/ppermute | solution.py:19
  289.6 5.0 %fusion.11 = f32[512,4,256]{0,2,1:T(8,128)} fusion(f32[5,512,4,256]{1,3,0,2:T(8,128)} %get-tuple-element.27, f32[512,1,2,2,256]{0,4,3,2,1:T(8,128)} %rev.19, f32[512,2,2,1,256]{0,4,2,1,3:T(8,128)S(1)} %rev.18, bf16[512,4,256]{0,2,1:T(8,128)(2,1)} %collective-permute-done.3, bf16[512,4,256]{0,2,1:T(8,128)(2,1)} %collective-permute-done.2), kind=kLoop, calls=%fused_computation.19 | loop fusion | flops 3145728 | bytes 10485760 | tf_op jit(solution)/shard_map/add | solution.py:83
  294.6 3.1 copy.53
  297.7 2.9 add_convert_fusion
  300.6 79.1 %reduce-scatter.6.cloned.1.call-done = bf16[16,5,32,256]{3,2,1,0:T(8,128)(2,1)} async-done(((bf16[16,5,256,256]{3,2,1,0:T(8,128)(2,1)}), bf16[16,5,32,256]{3,2,1,0:T(8,128)(2,1)}) %reduce-scatter.6.cloned.1.call-update) | async-done | bytes 1310736 | tf_op jit(solution)/shard_map/reduce_scatter | solution.py:91
  (49 shorter events, 23.3 us)
Async XLA Ops:
  8.0 27.5 %copy-start = (bf16[512,1024]{1,0:T(8,128)(2,1)S(1)}, bf16[512,1024]{1,0:T(8,128)(2,1)}, u32[]{:S(2)}) copy-start(bf16[512,1024]{1,0:T(8,128)(2,1)} %param.5) | copy-start | bytes 3145732
  8.0 104.6 %all-gather.3.cloned.1.call-start = ((), (), s32[]{:S(2)}) async-start(), calls=%async_computation.3 | async-start | bytes 11796480 | tf_op jit(solution)/shard_map/all_gather | solution.py:42
  8.7 124.8 %all-reduce.3.cloned.1.call-start = ((), (), s32[]{:S(2)}) async-start(), calls=%async_computation.4 | async-start | bytes 524288 | tf_op jit(solution)/shard_map/psum | solution.py:60
  25.6 0.8 copy-start.3
  28.8 113.3 %all-gather.5.cloned.1.call-start = ((), (), s32[]{:S(2)}) async-start(), calls=%async_computation.5 | async-start | bytes 2359296 | tf_op jit(solution)/shard_map/all_gather | solution.py:44
  29.6 168.7 %all-reduce.5.cloned.1.call-start = ((), (), s32[]{:S(2)}) async-start(), calls=%async_computation.6 | async-start | bytes 524288 | tf_op jit(solution)/shard_map/psum | solution.py:71
  32.5 27.8 %collective-permute-start = (bf16[512,4,256]{2,0,1:T(8,128)(2,1)}, bf16[512,4,256]{2,0,1:T(8,128)(2,1)}, u32[]{:S(2)}, u32[]{:S(2)}) collective-permute-start(bf16[512,4,256]{2,0,1:T(8,128)(2,1)} %copy.44), channel_id=1, source_target_pairs={{0,1},{1,0},{2,3},{3,2},{4,5},{5,4},{6,7},{7,6},{8,9},{9,8},{10,11... | collective-permute-start | bytes 3145736 | tf_op jit(solution)/shard_map/ppermute | solution.py:19
  34.0 28.6 %collective-permute-start.1 = (bf16[512,4,256]{2,0,1:T(8,128)(2,1)}, bf16[512,4,256]{2,0,1:T(8,128)(2,1)}, u32[]{:S(2)}, u32[]{:S(2)}) collective-permute-start(bf16[512,4,256]{2,0,1:T(8,128)(2,1)} %copy.44), channel_id=1, source_target_pairs={{0,2},{2,0},{1,3},{3,1},{4,6},{6,4},{5,7},{7,5},{8,10},{10,8},{9,1... | collective-permute-start | bytes 3145736 | tf_op jit(solution)/shard_map/ppermute | solution.py:19
  142.1 12.1 %copy-start.7 = (bf16[256,4096]{1,0:T(8,128)(2,1)S(1)}, bf16[256,4096]{1,0:T(8,128)(2,1)}, u32[]{:S(2)}) copy-start(bf16[256,4096]{1,0:T(8,128)(2,1)} %all-gather.5.cloned.1.call-done) | copy-start | bytes 6291460
  152.1 2.1 copy-start.1
  154.2 46.7 %copy-start.6 = (bf16[512,256]{1,0:T(8,128)(2,1)S(1)}, bf16[512,256]{1,0:T(8,128)(2,1)}, u32[]{:S(2)}) copy-start(bf16[512,256]{1,0:T(8,128)(2,1)} %all-reduce.3.cloned.1.call-done) | copy-start | bytes 786436
  156.2 144.3 %reduce-scatter.10.cloned.1.call-start = ((), (), s32[]{:S(2)}) async-start(), calls=%async_computation.9 | async-start | bytes 589824
  200.7 99.9 %reduce-scatter.8.cloned.1.call-start = ((), (), s32[]{:S(2)}) async-start(), calls=%async_computation.8 | async-start | bytes 2359296 | tf_op jit(solution)/shard_map/reduce_scatter | solution.py:97
  205.8 173.8 %reduce-scatter.6.cloned.1.call-start = ((), (), s32[]{:S(2)}) async-start(), calls=%async_computation.7 | async-start | bytes 11796480 | tf_op jit(solution)/shard_map/reduce_scatter | solution.py:91
  263.5 24.7 %collective-permute-start.2 = (bf16[512,4,256]{0,2,1:T(8,128)(2,1)}, bf16[512,4,256]{0,2,1:T(8,128)(2,1)}, u32[]{:S(2)}, u32[]{:S(2)}) collective-permute-start(bf16[512,4,256]{0,2,1:T(8,128)(2,1)} %get-tuple-element.24), channel_id=1, source_target_pairs={{0,1},{1,0},{2,3},{3,2},{4,5},{5,4},{6,7},{7,6},{8,9},{9,8},{10,11... | collective-permute-start | bytes 3145736 | tf_op jit(solution)/shard_map/ppermute | solution.py:19
  265.0 24.6 %collective-permute-start.3 = (bf16[512,4,256]{0,2,1:T(8,128)(2,1)}, bf16[512,4,256]{0,2,1:T(8,128)(2,1)}, u32[]{:S(2)}, u32[]{:S(2)}) collective-permute-start(bf16[512,4,256]{0,2,1:T(8,128)(2,1)} %get-tuple-element.25), channel_id=1, source_target_pairs={{0,2},{2,0},{1,3},{3,1},{4,6},{6,4},{5,7},{7,5},{8,10},{10,8},{9,1... | collective-permute-start | bytes 3145736 | tf_op jit(solution)/shard_map/ppermute | solution.py:19
  270.2 4.9 %copy-start.4 = (bf16[1024,256]{1,0:T(8,128)(2,1)S(1)}, bf16[1024,256]{1,0:T(8,128)(2,1)}, u32[]{:S(2)}) copy-start(bf16[1024,256]{1,0:T(8,128)(2,1)} %copy-done.3) | copy-start | bytes 1572868
  270.2 4.9 %copy-start.5 = (bf16[512,256]{1,0:T(8,128)(2,1)S(1)}, bf16[512,256]{1,0:T(8,128)(2,1)}, u32[]{:S(2)}) copy-start(bf16[512,256]{1,0:T(8,128)(2,1)} %all-reduce.5.cloned.1.call-done) | copy-start | bytes 786436
  294.6 3.1 copy-start.2
Sparse Core Ops, SparseCore 0:
  10.4 102.0 all-gather.2
  114.3 27.8 all-gather.4
  200.8 30.9 reduce-scatter.9
  234.6 33.9 reduce-scatter.7
  271.5 108.0 reduce-scatter.5
Sparse Core Ops, SparseCore 1:
  28.9 46.1 all-reduce.2
  156.3 41.9 all-reduce.4
where the time goes:
time: 388 us; the launch traced here: 387 us
  waiting for transfers between devices  200 us (52%)
  local copies, waits for them, and re-layouts  82.8 us (21%)
  matrix products  58.3 us (15%)
  blocking collectives  16.8 us (4%)
  between operations  15.3 us (4%)
  other arithmetic  7.92 us (2%)
  starting transfers between devices  5.51 us (1%)
    reduce_scatter x1, waiting for transfers between devices, per_device(): lax.psum_scatter(grad_weight.astype(jnp.bfloat16), 'dp', scatter_dimensio...  79.1 us
    all_gather x1, waiting for transfers between devices, per_device(): lax.all_gather(butterfly, 'dp', axis=2, tiled=True)  47.8 us
    psum x1, waiting for transfers between devices, per_device(): grad_low = lax.psum(low_back.astype(jnp.bfloat16), 'tensor')  42 us
    ppermute x4, waiting for transfers between devices, swapped(): return lax.ppermute(block, axis, route)  21.2 us
    all_gather x1, blocking collectives, per_device(): lax.all_gather(left_factor, 'dp', axis=0, tiled=True)  16.8 us
    reshape x2, local copies, waits for them, and re-layouts, per_device(): grad_wide = grad_pre.reshape(rows_here, blocks_here, group_ratio, BLK)  15.4 us
    convert_element_type x1, local copies, waits for them, and re-layouts, per_device(): grad_weight.astype(jnp.bfloat16)  15.2 us
    dot_general x1, matrix products, per_device(): jnp.einsum('tqro,qrkio->ktqi', grad_wide, weight_blocks, preferred_elemen...  12.8 us
  transfers between devices with their start and end apart: 11, of which 7 were waited for; matrix products, arithmetic and copies ran while one was open for 34% of the time, Pallas kernels for 0%

commit v1 on v0

--- a/solution.py
+++ b/solution.py
@@ -68,7 +68,7 @@
     )
     grad_weight = grad_weight.reshape(hidden_blocks, LOG + 1, BLK, BLK)
     low_back = jnp.einsum("th,rh->tr", grad_pre, right_full, preferred_element_type=jnp.float32)
-    grad_low = lax.psum(low_back.astype(jnp.bfloat16), "tensor")
+    grad_low = jnp.sum(lax.all_gather(low_back.astype(jnp.bfloat16), "tensor"), axis=0)
     grad_first = jnp.einsum("td,tr->dr", tokens, grad_low, preferred_element_type=jnp.float32)
     grad_second = jnp.einsum("tr,th->rh", low_rank, grad_pre, preferred_element_type=jnp.float32)
     returned = jnp.einsum(

time: 388 us -> 372 us (0.959)
  waiting for transfers between devices: 200 us -> 188 us
    psum x1 -> x0, waiting for transfers between devices: 42 us -> none  [per_device(): grad_low = lax.psum(low_back.astype(jnp.bfloat16), 'tensor')]
    all_gather x0 -> x1, waiting for transfers between devices: none -> 26 us  [per_device(): lax.all_gather(low_back.astype(jnp.bfloat16), 'tensor')]
    unnamed x22 -> x18, local copies, waits for them, and re-layouts: 12 us -> 12.1 us
where the time goes in v1:
time: 372 us; the launch traced here: 371 us
  waiting for transfers between devices  188 us (51%)
  local copies, waits for them, and re-layouts  81.6 us (22%)
  matrix products  56.1 us (15%)
  blocking collectives  16.8 us (5%)
  between operations  15.3 us (4%)
  other arithmetic  7.7 us (2%)
  starting transfers between devices  5.5 us (1%)
    reduce_scatter x1, waiting for transfers between devices, per_device(): lax.psum_scatter(grad_weight.astype(jnp.bfloat16), 'dp', scatter_dimensio...  80.8 us
    all_gather x1, waiting for transfers between devices, per_device(): lax.all_gather(butterfly, 'dp', axis=2, tiled=True)  47.8 us
    all_gather x1, waiting for transfers between devices, per_device(): lax.all_gather(low_back.astype(jnp.bfloat16), 'tensor')  26 us
    ppermute x4, waiting for transfers between devices, swapped(): return lax.ppermute(block, axis, route)  23.4 us
    all_gather x1, blocking collectives, per_device(): lax.all_gather(left_factor, 'dp', axis=0, tiled=True)  16.8 us
    reshape x2, local copies, waits for them, and re-layouts, per_device(): grad_wide = grad_pre.reshape(rows_here, blocks_here, group_ratio, BLK)  15.4 us
    convert_element_type x1, local copies, waits for them, and re-layouts, per_device(): grad_weight.astype(jnp.bfloat16)  15.1 us
    dot_general x1, matrix products, per_device(): jnp.einsum('tqro,qrkio->ktqi', grad_wide, weight_blocks, preferred_elemen...  12.7 us
  transfers between devices with their start and end apart: 11, of which 7 were waited for; matrix products, arithmetic and copies ran while one was open for 34% of the time, Pallas kernels for 0%

profile of v1, /device:TPU:0, one launch (start us, length us, event | category | flops | bytes accessed | tf_op | source)
XLA Modules:
  0.0 371.0 jit_solution(3722732126414042587)
XLA Ops:
  8.8 16.8 %all_gather.16 = bf16[1024,256]{1,0:T(8,128)(2,1)S(1)} all-gather(bf16[128,256]{1,0:T(8,128)(2,1)} %param.7), channel_id=1, replica_groups=mesh['dp'=8,'tensor'=4] {'dp'}, dimensions={0}, use_global_device_ids=true | all-gather | bytes 589824 | tf_op jit(solution)/shard_map/all_gather | solution.py:43
  26.4 2.4 convolution_convert_fusion.4
  35.5 1.6 reshape_reshape.7
  39.1 2.3 copy.42
  42.8 2.4 copy.41
  45.2 2.3 rev.16
  48.5 2.3 constant_dynamic-update-slice_fusion.1
  51.8 8.5 %collective-permute-done = bf16[512,4,256]{2,0,1:T(8,128)(2,1)} collective-permute-done((bf16[512,4,256]{2,0,1:T(8,128)(2,1)}, bf16[512,4,256]{2,0,1:T(8,128)(2,1)}, u32[]{:S(2)}, u32[]{:S(2)}) %collective-permute-start) | collective-permute-done | bytes 1048608 | tf_op jit(solution)/shard_map/ppermute | solution.py:19
  60.3 2.3 bitcast_dynamic-update-slice_fusion.1
  62.6 2.3 bitcast_dynamic-update-slice_fusion
  64.8 47.8 %all-gather.5.cloned.1.call-done = bf16[16,5,256,256]{3,2,1,0:T(8,128)(2,1)} async-done(((bf16[16,5,32,256]{3,2,1,0:T(8,128)(2,1)}), bf16[16,5,256,256]{3,2,1,0:T(8,128)(2,1)}) %all-gather.5.cloned.1.call-update) | async-done | bytes 10485776 | tf_op jit(solution)/shard_map/all_gather | solution.py:42
  112.6 12.0 %fusion.6 = f32[4,512,4,256,1]{1,3,4,2,0:T(8,128)} fusion(bf16[4,4,5,256,256]{4,3,2,1,0:T(8,128)(2,1)} %bitcast.95, bf16[5,512,4,256]{3,1,0,2:T(8,128)(2,1)} %bitcast_dynamic-update-slice_fusion), kind=kOutput, calls=%fused_computation.11 | convolution fusion | flops 5368709120 | bytes 24117248 | tf_op jit(solution)/shard_map/ktqi,qrkio->tqro/dot_general | solution.py:55
  124.6 9.0 %copy.48 = f32[512,4096]{1,0:T(8,128)} copy(f32[512,4096]{0,1:T(8,128)} %bitcast.89) | data formatting | bytes 16777216 | tf_op jit(solution)/shard_map/reshape | solution.py:58
  133.5 8.6 %all-gather.7.cloned.1.call-done = bf16[256,4096]{1,0:T(8,128)(2,1)} async-done(((bf16[32,4096]{1,0:T(8,128)(2,1)}), bf16[256,4096]{1,0:T(8,128)(2,1)}) %all-gather.7.cloned.1.call-update) | async-done | bytes 2097168 | tf_op jit(solution)/shard_map/all_gather | solution.py:44
  142.1 10.0 %fusion.4 = (bf16[512,4096]{1,0:T(8,128)(2,1)S(1)}, bf16[512,4096]{1,0:T(8,128)(2,1)}) fusion(bf16[512,4096]{1,0:T(8,128)(2,1)} %param.9, f32[512,4096]{1,0:T(8,128)} %copy.48, bf16[512,256]{1,0:T(8,128)(2,1)} %all-reduce.2.cloned.1.call-done, bf16[256,4096]{1,0:T(8,128)(2,1)} %all-gather.7.cloned.1.call-done), kind=kOutput, calls=%fused_computation.5 | convolution fusion | flops 1103101952 | bytes 23330816 | tf_op jit(solution)/shard_map/dot_general | solution.py:61
  152.1 2.1 copy-done.1
  154.2 2.0 convolution_convert_fusion.3
  156.3 26.0 %all-gather.9.cloned.1.call-done = bf16[2048,256]{1,0:T(8,128)(2,1)} async-done(((bf16[512,256]{1,0:T(8,128)(2,1)}), bf16[2048,256]{1,0:T(8,128)(2,1)}) %all-gather.9.cloned.1.call-update) | async-done | bytes 1048592 | tf_op jit(solution)/shard_map/all_gather | solution.py:71
  185.5 4.8 %convolution_convert_fusion.1 = bf16[256,4096]{1,0:T(8,128)(2,1)} fusion(bf16[512,256]{1,0:T(8,128)(2,1)S(1)} %copy-done.4, bf16[512,4096]{1,0:T(8,128)(2,1)} %copy-done.1), kind=kOutput, calls=%fused_computation.13 | convolution fusion | flops 1074790400 | bytes 6553600 | tf_op jit(solution)/shard_map/tr,th->rh/dot_general | solution.py:73
  190.4 7.9 %reshape.38 = bf16[512,4,4,256]{3,2,1,0:T(4,128)(2,1)} reshape(bf16[512,4096]{1,0:T(8,128)(2,1)} %copy-done.1) | data formatting | bytes 8388608 | tf_op jit(solution)/shard_map/reshape | solution.py:65
  198.3 7.5 %copy.62 = bf16[512,4,4,256,1]{0,3,4,2,1:T(8,128)(2,1)} copy(bf16[512,4,4,256,1]{3,2,1,0,4:T(4,128)(2,1)} %bitcast.84) | data formatting | bytes 8388608 | tf_op jit(solution)/shard_map/reshape | solution.py:65
  205.8 11.3 %convolution_convert_fusion = bf16[4,4,256,5,256]{4,2,3,1,0:T(8,128)(2,1)} fusion(bf16[512,4,4,256,1]{0,3,4,2,1:T(8,128)(2,1)} %copy.62, bf16[5,512,4,256]{3,1,0,2:T(8,128)(2,1)} %bitcast_dynamic-update-slice_fusion), kind=kOutput, calls=%fused_computation.9 | convolution fusion | flops 5373952000 | bytes 19922944 | tf_op jit(solution)/shard_map/ktqi,tqro->qrkio/dot_general | solution.py:66
  217.1 15.1 %copy.55 = bf16[16,5,256,256]{3,2,1,0:T(8,128)(2,1)} copy(bf16[16,5,256,256]{2,3,1,0:T(8,128)(2,1)} %bitcast.85) | data formatting | bytes 20971520 | tf_op jit(solution)/shard_map/convert_element_type | solution.py:92
  232.3 12.7 %fusion.14 = (bf16[5,512,4,256]{1,3,0,2:T(8,128)(2,1)}, f32[5,512,4,256]{1,3,0,2:T(8,128)}) fusion(bf16[512,4,4,256,1]{0,3,4,2,1:T(8,128)(2,1)} %copy.62, bf16[4,4,5,256,256]{4,3,2,1,0:T(8,128)(2,1)} %bitcast.96), kind=kOutput, calls=%fused_computation.33 | convolution fusion | flops 5371330560 | bytes 30408704 | tf_op jit(solution)/shard_map/tqro,qrkio->ktqi/dot_general | solution.py:74
  245.0 3.0 slice_bitcast_fusion.2
  250.1 4.6 %fusion.13 = (f32[1,512,4,256]{1,3,0,2:T(8,128)}, f32[1,512,4,256]{1,3,0,2:T(8,128)}) fusion(f32[5,512,4,256]{1,3,0,2:T(8,128)} %get-tuple-element.27), kind=kLoop, calls=%fused_computation.32 | loop fusion | bytes 8388608 | tf_op jit(solution)/shard_map/slice | solution.py:79
  254.7 1.8 rev.18
  256.5 3.1 rev.19
  259.6 13.7 %collective-permute-done.2 = bf16[512,4,256]{0,2,1:T(8,128)(2,1)} collective-permute-done((bf16[512,4,256]{0,2,1:T(8,128)(2,1)}, bf16[512,4,256]{0,2,1:T(8,128)(2,1)}, u32[]{:S(2)}, u32[]{:S(2)}) %collective-permute-start.2) | collective-permute-done | bytes 1048608 | tf_op jit(solution)/shard_map/ppermute | solution.py:19
  274.4 5.0 %fusion.11 = f32[512,4,256]{0,2,1:T(8,128)} fusion(f32[5,512,4,256]{1,3,0,2:T(8,128)} %get-tuple-element.27, f32[512,1,2,2,256]{0,4,3,2,1:T(8,128)} %rev.19, f32[512,2,2,1,256]{0,4,2,1,3:T(8,128)S(1)} %rev.18, bf16[512,4,256]{0,2,1:T(8,128)(2,1)} %collective-permute-done.3, bf16[512,4,256]{0,2,1:T(8,128)(2,1)} %collective-permute-done.2), kind=kLoop, calls=%fused_computation.19 | loop fusion | flops 3145728 | bytes 10485760 | tf_op jit(solution)/shard_map/add | solution.py:83
  279.4 1.9 copy.53
  283.1 80.8 %reduce-scatter.6.cloned.1.call-done = bf16[16,5,32,256]{3,2,1,0:T(8,128)(2,1)} async-done(((bf16[16,5,256,256]{3,2,1,0:T(8,128)(2,1)}), bf16[16,5,32,256]{3,2,1,0:T(8,128)(2,1)}) %reduce-scatter.6.cloned.1.call-update) | async-done | bytes 1310736 | tf_op jit(solution)/shard_map/reduce_scatter | solution.py:91
  (46 shorter events, 22.0 us)
Async XLA Ops:
  8.0 27.5 %copy-start = (bf16[512,1024]{1,0:T(8,128)(2,1)S(1)}, bf16[512,1024]{1,0:T(8,128)(2,1)}, u32[]{:S(2)}) copy-start(bf16[512,1024]{1,0:T(8,128)(2,1)} %param.5) | copy-start | bytes 3145732
  8.0 104.6 %all-gather.5.cloned.1.call-start = ((), (), s32[]{:S(2)}) async-start(), calls=%async_computation.3 | async-start | bytes 11796480 | tf_op jit(solution)/shard_map/all_gather | solution.py:42
  8.7 124.8 %all-reduce.2.cloned.1.call-start = ((), (), s32[]{:S(2)}) async-start(), calls=%async_computation.4 | async-start | bytes 524288 | tf_op jit(solution)/shard_map/psum | solution.py:60
  25.6 0.8 copy-start.2
  28.8 113.3 %all-gather.7.cloned.1.call-start = ((), (), s32[]{:S(2)}) async-start(), calls=%async_computation.5 | async-start | bytes 2359296 | tf_op jit(solution)/shard_map/all_gather | solution.py:44
  29.6 152.7 %all-gather.9.cloned.1.call-start = ((), (), s32[]{:S(2)}) async-start(), calls=%async_computation.8 | async-start | bytes 1310720 | tf_op jit(solution)/shard_map/all_gather | solution.py:71
  32.5 27.8 %collective-permute-start = (bf16[512,4,256]{2,0,1:T(8,128)(2,1)}, bf16[512,4,256]{2,0,1:T(8,128)(2,1)}, u32[]{:S(2)}, u32[]{:S(2)}) collective-permute-start(bf16[512,4,256]{2,0,1:T(8,128)(2,1)} %copy.44), channel_id=1, source_target_pairs={{0,1},{1,0},{2,3},{3,2},{4,5},{5,4},{6,7},{7,6},{8,9},{9,8},{10,11... | collective-permute-start | bytes 3145736 | tf_op jit(solution)/shard_map/ppermute | solution.py:19
  34.0 28.6 %collective-permute-start.1 = (bf16[512,4,256]{2,0,1:T(8,128)(2,1)}, bf16[512,4,256]{2,0,1:T(8,128)(2,1)}, u32[]{:S(2)}, u32[]{:S(2)}) collective-permute-start(bf16[512,4,256]{2,0,1:T(8,128)(2,1)} %copy.44), channel_id=1, source_target_pairs={{0,2},{2,0},{1,3},{3,1},{4,6},{6,4},{5,7},{7,5},{8,10},{10,8},{9,1... | collective-permute-start | bytes 3145736 | tf_op jit(solution)/shard_map/ppermute | solution.py:19
  142.1 12.1 %copy-start.5 = (bf16[256,4096]{1,0:T(8,128)(2,1)S(1)}, bf16[256,4096]{1,0:T(8,128)(2,1)}, u32[]{:S(2)}) copy-start(bf16[256,4096]{1,0:T(8,128)(2,1)} %all-gather.7.cloned.1.call-done) | copy-start | bytes 6291460
  152.1 2.1 copy-start.1
  154.2 31.3 %copy-start.4 = (bf16[512,256]{1,0:T(8,128)(2,1)S(1)}, bf16[512,256]{1,0:T(8,128)(2,1)}, u32[]{:S(2)}) copy-start(bf16[512,256]{1,0:T(8,128)(2,1)} %all-reduce.2.cloned.1.call-done) | copy-start | bytes 786436
  156.2 126.9 %reduce-scatter.10.cloned.1.call-start = ((), (), s32[]{:S(2)}) async-start(), calls=%async_computation.9 | async-start | bytes 589824
  185.3 97.8 %reduce-scatter.8.cloned.1.call-start = ((), (), s32[]{:S(2)}) async-start(), calls=%async_computation.7 | async-start | bytes 2359296 | tf_op jit(solution)/shard_map/reduce_scatter | solution.py:97
  190.3 173.5 %reduce-scatter.6.cloned.1.call-start = ((), (), s32[]{:S(2)}) async-start(), calls=%async_computation.6 | async-start | bytes 11796480 | tf_op jit(solution)/shard_map/reduce_scatter | solution.py:91
  248.0 25.2 %collective-permute-start.2 = (bf16[512,4,256]{0,2,1:T(8,128)(2,1)}, bf16[512,4,256]{0,2,1:T(8,128)(2,1)}, u32[]{:S(2)}, u32[]{:S(2)}) collective-permute-start(bf16[512,4,256]{0,2,1:T(8,128)(2,1)} %get-tuple-element.24), channel_id=1, source_target_pairs={{0,1},{1,0},{2,3},{3,2},{4,5},{5,4},{6,7},{7,6},{8,9},{9,8},{10,11... | collective-permute-start | bytes 3145736 | tf_op jit(solution)/shard_map/ppermute | solution.py:19
  249.5 24.9 %collective-permute-start.3 = (bf16[512,4,256]{0,2,1:T(8,128)(2,1)}, bf16[512,4,256]{0,2,1:T(8,128)(2,1)}, u32[]{:S(2)}, u32[]{:S(2)}) collective-permute-start(bf16[512,4,256]{0,2,1:T(8,128)(2,1)} %get-tuple-element.25), channel_id=1, source_target_pairs={{0,2},{2,0},{1,3},{3,1},{4,6},{6,4},{5,7},{7,5},{8,10},{10,8},{9,1... | collective-permute-start | bytes 3145736 | tf_op jit(solution)/shard_map/ppermute | solution.py:19
  259.6 21.8 %copy-start.3 = (bf16[1024,256]{1,0:T(8,128)(2,1)S(1)}, bf16[1024,256]{1,0:T(8,128)(2,1)}, u32[]{:S(2)}) copy-start(bf16[1024,256]{1,0:T(8,128)(2,1)} %copy-done.2) | copy-start | bytes 1572868
Sparse Core Ops, SparseCore 0:
  10.4 102.0 all-gather.4
  114.3 27.8 all-gather.6
  185.4 30.9 reduce-scatter.9
  219.1 33.9 reduce-scatter.7
  255.9 107.9 reduce-scatter.5
Sparse Core Ops, SparseCore 1:
  28.9 46.1 all-reduce.1
  156.3 25.9 all-gather.8
